TPU v7x, 256 devices: a whole 4x4x8 slice. The times are simulated.
256 devices in a mesh: neur: 32 (over y, z_hi, core), tm: 8 (over x, z_lo).
Axes of the slice: x: 4, y: 4, z: 8 (z_hi: 4, z_lo: 2; z = z_hi * 2 + z_lo), core: 2. Of those that a mesh axis runs over, the one named last changes fastest.
Arguments:
- spikes: int32 [1024, 262144], P(None, ('neur', 'tm')), may hold values from 0 to 9
- held_in: int32 [262144], P(('neur', 'tm')), may hold values 0 or 1
- readin_weight: bfloat16 [262144, 1024], P(('neur', 'tm')), may hold values from -0.01171875 to 0.01171875
- qkv_weight: bfloat16 [1024, 3, 1024], P(None, None, 'tm'), may hold values from -0.1875 to 0.1875
- out_weight: bfloat16 [1024, 1024], P('tm'), may hold values from -0.1875 to 0.1875
- up_weight: bfloat16 [1024, 4096], P(None, 'tm'), may hold values from -0.1875 to 0.1875
- down_weight: bfloat16 [4096, 1024], P('tm'), may hold values from -0.09375 to 0.09375
- norm_gain: float32 [1024], replicated, may hold values from 0.25 to 1.75
- mlp_gain: float32 [1024], replicated, may hold values from 0.25 to 1.75
- final_gain: float32 [1024], replicated, may hold values from 0.25 to 1.75
- readout_weight: bfloat16 [262144, 1024], P(('neur', 'tm')), may hold values from -0.1875 to 0.1875
- readout_bias: float32 [262144], P(('neur', 'tm')), may hold values from -3 to 3
Outputs:
- latents: bfloat16 [1024, 1024], P('neur')
- neuron_bits: float32 [262144], P(('neur', 'tm'))
- bits_per_spike: float32 [], replicated
All inputs are finite; a program needn't handle non-finite values. No bound on the sum of `held_in` on one device may be relied on, other than what follows from the above.
Results may differ from a plain program's by a relative error of at most 0.006.
Values may be sent and summed in bfloat16 or wider, within the bound.
No kernel may reach another device: no remote copies, remote signals or barrier semaphores. Data moves between devices by JAX's collectives and lax.ppermute only.
A program may use at most 64 MiB of HBM per device.

v0:
```python
import math
import jax
import jax.numpy as jnp
from jax import lax
from jax.sharding import PartitionSpec as P

HEAD_DIM = 128


def normed(values, gain_vec):
    return values * lax.rsqrt(jnp.mean(values * values, -1, keepdims=True) + 1e-05) * gain_vec


def on_device(
    spikes,
    held_in,
    readin_weight,
    qkv_weight,
    out_weight,
    up_weight,
    down_weight,
    norm_gain,
    mlp_gain,
    final_gain,
    readout_weight,
    readout_bias,
):
    frames_all = spikes.shape[0]
    rows_here = frames_all // lax.axis_size("neur")
    masked = (spikes * held_in[None, :]).astype(jnp.bfloat16)
    heldout = (1 - held_in).astype(jnp.float32)
    counts = jnp.sum(spikes, 0).astype(jnp.float32)
    partial_sum = jnp.dot(masked, readin_weight, preferred_element_type=jnp.float32)
    summed = lax.psum(partial_sum, ("neur", "tm"))
    stream = lax.dynamic_slice_in_dim(summed, lax.axis_index("neur") * rows_here, rows_here, 0)
    model_dim = stream.shape[1]
    head_cols = qkv_weight.shape[2]
    local_heads = head_cols // HEAD_DIM
    attn_in = normed(stream, norm_gain).astype(jnp.bfloat16)
    projected = jnp.dot(
        attn_in, qkv_weight.reshape(model_dim, 3 * head_cols), preferred_element_type=jnp.float32
    ).astype(jnp.bfloat16)
    queries = projected[:, :head_cols].reshape(rows_here, local_heads, HEAD_DIM)
    keys_local = projected[:, head_cols : 2 * head_cols]
    values_local = projected[:, 2 * head_cols :]
    scaling = 1.0 / math.sqrt(HEAD_DIM)
    key_rows = lax.all_gather(keys_local, "neur", axis=0, tiled=True).reshape(
        -1, local_heads, HEAD_DIM
    )
    value_rows = lax.all_gather(values_local, "neur", axis=0, tiled=True).reshape(
        -1, local_heads, HEAD_DIM
    )
    scores = (
        jnp.einsum("qhd,khd->hqk", queries, key_rows, preferred_element_type=jnp.float32) * scaling
    )
    weights = jnp.exp(scores)
    numerator = jnp.einsum(
        "hqk,khd->qhd", weights.astype(jnp.bfloat16), value_rows, preferred_element_type=jnp.float32
    )
    denominator = jnp.sum(weights, -1).T
    numerator, denominator = (numerator, denominator)
    heads_out = (
        (numerator / denominator[:, :, None]).astype(jnp.bfloat16).reshape(rows_here, head_cols)
    )
    attn_part = jnp.dot(heads_out, out_weight, preferred_element_type=jnp.float32)
    mixed_state = stream + lax.psum(attn_part, "tm")
    mlp_in = normed(mixed_state, mlp_gain).astype(jnp.bfloat16)
    hidden_act = jax.nn.gelu(jnp.dot(mlp_in, up_weight, preferred_element_type=jnp.float32)).astype(
        jnp.bfloat16
    )
    mlp_part = jnp.dot(hidden_act, down_weight, preferred_element_type=jnp.float32)
    final_state = mixed_state + lax.psum(mlp_part, "tm")
    latents = normed(final_state, final_gain).astype(jnp.bfloat16)
    log_rate = (
        lax.dot_general(
            lax.all_gather(latents, "neur", axis=0, tiled=True),
            readout_weight,
            (((1,), (1,)), ((), ())),
            preferred_element_type=jnp.float32,
        )
        + readout_bias[None, :]
    )
    observed = spikes.astype(jnp.float32)
    model_ll = jnp.sum(observed * log_rate - jnp.exp(log_rate), 0)
    null_ll = counts * jnp.log((counts + 1.0) / frames_all) - (counts + 1.0)
    gained = heldout * (model_ll - null_ll)
    neuron_bits = gained / (math.log(2.0) * (counts + 1.0))
    score_sum, spike_sum = lax.psum((jnp.sum(gained), jnp.sum(heldout * counts)), ("neur", "tm"))
    bits_total = score_sum / (math.log(2.0) * (1.0 + spike_sum))
    return (latents, neuron_bits, bits_total)


def solution(mesh):
    in_specs = (
        P(None, ("neur", "tm")),
        P(("neur", "tm")),
        P(("neur", "tm"), None),
        P(None, None, "tm"),
        P("tm", None),
        P(None, "tm"),
        P("tm", None),
        P(),
        P(),
        P(),
        P(("neur", "tm"), None),
        P(("neur", "tm")),
    )
    out_specs = (P("neur", None), P(("neur", "tm")), P())
    return jax.shard_map(
        on_device, mesh=mesh, in_specs=in_specs, out_specs=out_specs, check_vma=False
    )
```

profile of v0, /device:TPU:1, one launch (start us, length us, event | category | flops | bytes accessed | tf_op | source)
XLA Modules:
  0.0 675.9 jit_solution(17022954513759164385)
XLA Ops:
  7.2 0.0 copy-start
  7.2 0.0 all-reduce.5.cloned.1.call-start
  7.2 1.5 copy-done
  8.8 6.5 fusion
  15.3 0.0 copy-start.2
  15.3 0.0 copy-start.1
  15.3 0.0 copy-start.5
  15.3 0.0 all-reduce.5.cloned.1.call-update
  15.3 0.0 copy-start.3
  15.3 0.0 all-reduce.7.cloned.1.call-start
  15.4 1.4 copy.15
  16.8 269.4 %all-reduce.5.cloned.1.call-done = f32[1024,1024]{1,0:T(8,128)} async-done(((f32[1024,1024]{1,0:T(8,128)}), f32[1024,1024]{1,0:T(8,128)}) %all-reduce.5.cloned.1.call-update) | async-done | bytes 4194320 | tf_op jit(solution)/shard_map/psum | solution.py:34
  286.2 1.0 multiply_reduce_fusion.2
  287.2 0.0 copy-done.2
  287.2 1.2 convolution_convert_fusion
  288.5 42.8 %all_gather.10 = bf16[1024,128]{1,0:T(8,128)(2,1)S(1)} all-gather(bf16[32,128]{1,0:T(8,128)(2,1)S(1)} %get-tuple-element.11), channel_id=1, replica_groups=mesh['neur'=32,'tm'=8] {'neur'}, dimensions={0}, use_global_device_ids=true | all-gather | bytes 270336 | tf_op jit(solution)/shard_map/all_gather | solution.py:47
  331.3 0.3 fusion.38
  331.6 42.1 %all_gather.9 = bf16[1024,128]{1,0:T(8,128)(2,1)S(1)} all-gather(bf16[32,128]{1,0:T(8,128)(2,1)S(1)} %get-tuple-element.12), channel_id=1, replica_groups=mesh['neur'=32,'tm'=8] {'neur'}, dimensions={0}, use_global_device_ids=true | all-gather | bytes 270336 | tf_op jit(solution)/shard_map/all_gather | solution.py:50
  373.7 0.0 copy-done.1
  373.7 0.0 copy-start.6
  373.7 0.9 fusion.6
  374.6 0.0 all-reduce.7.cloned.1.call-update
  374.6 0.0 all-reduce.9.cloned.1.call-start
  374.7 67.4 %all-reduce.7.cloned.1.call-done = f32[32,1024]{1,0:T(8,128)} async-done(((f32[32,1024]{1,0:T(8,128)}), f32[32,1024]{1,0:T(8,128)}) %all-reduce.7.cloned.1.call-update) | async-done | bytes 131088 | tf_op jit(solution)/shard_map/psum | solution.py:66
  442.1 1.1 multiply_reduce_fusion.1
  443.2 0.0 copy-done.5
  443.2 2.8 fusion.16
  446.0 0.0 all-reduce.9.cloned.1.call-update
  446.0 0.0 all-gather.2.cloned.1.call-start
  446.1 76.6 %all-reduce.9.cloned.1.call-done = f32[32,1024]{1,0:T(8,128)} async-done(((f32[32,1024]{1,0:T(8,128)}), f32[32,1024]{1,0:T(8,128)}) %all-reduce.9.cloned.1.call-update) | async-done | bytes 131088 | tf_op jit(solution)/shard_map/psum | solution.py:72
  522.6 1.0 multiply_reduce_fusion
  523.7 0.0 copy-done.3
  523.7 0.7 multiply_convert_fusion.2
  524.4 0.0 all-gather.2.cloned.1.call-update
  524.4 2.5 reduce_sum.77
  526.9 0.0 copy-start.4
  526.9 58.2 %all-gather.2.cloned.1.call-done = bf16[1024,1024]{1,0:T(8,128)(2,1)} async-done(((bf16[32,1024]{1,0:T(8,128)(2,1)}), bf16[1024,1024]{1,0:T(8,128)(2,1)}) %all-gather.2.cloned.1.call-update) | async-done | bytes 2097168 | tf_op jit(solution)/shard_map/all_gather | solution.py:76
  585.1 0.0 copy-done.6
  585.1 6.2 subtract_reduce_fusion
  591.3 0.0 copy-done.4
  591.3 1.3 multiply_reduce_fusion.3
  592.6 74.4 %all-reduce = (f32[]{:T(128)}, f32[]{:T(128)}) all-reduce(f32[]{:T(128)} %get-tuple-element.4, f32[]{:T(128)} %get-tuple-element.3), channel_id=1, replica_groups=mesh['neur'=32,'tm'=8] {'neur','tm'}, use_global_device_ids=true, to_apply=%region_10.0 | all-reduce | flops 2 | bytes 16 | tf_op jit(solution)/shard_map/psum | solution.py:88
  (4 shorter events, 0.0 us)
Async XLA Ops:
  7.2 1.6 copy-start
  7.2 279.0 %all-reduce.5.cloned.1.call-start = ((), (), s32[]{:S(2)}) async-start(), calls=%async_computation | async-start | bytes 8388608 | tf_op jit(solution)/shard_map/psum | solution.py:34
  15.3 271.9 %copy-start.2 = (f32[1024]{0:T(1024)S(1)}, f32[1024]{0:T(1024)}, u32[]{:S(2)}) copy-start(f32[1024]{0:T(1024)} %param.19) | copy-start | bytes 12292
  15.3 358.4 %copy-start.1 = (bf16[128,1024]{1,0:T(8,128)(2,1)S(1)}, bf16[128,1024]{1,0:T(8,128)(2,1)}, u32[]{:S(2)}) copy-start(bf16[128,1024]{1,0:T(8,128)(2,1)} %param.16) | copy-start | bytes 786436
  15.3 428.0 %copy-start.5 = (f32[1024]{0:T(1024)S(1)}, f32[1024]{0:T(1024)}, u32[]{:S(2)}) copy-start(f32[1024]{0:T(1024)} %param.20) | copy-start | bytes 12292
  15.3 508.4 %copy-start.3 = (f32[1024]{0:T(1024)S(1)}, f32[1024]{0:T(1024)}, u32[]{:S(2)}) copy-start(f32[1024]{0:T(1024)} %param.21) | copy-start | bytes 12292
  15.3 426.8 %all-reduce.7.cloned.1.call-start = ((), (), s32[]{:S(2)}) async-start(), calls=%async_computation.1 | async-start | bytes 262144 | tf_op jit(solution)/shard_map/psum | solution.py:66
  373.7 211.5 %copy-start.6 = (f32[1024]{0:T(1024)S(1)}, f32[1024]{0:T(1024)}, u32[]{:S(2)}) copy-start(f32[1024]{0:T(1024)} %param.23) | copy-start | bytes 12292
  374.6 148.0 %all-reduce.9.cloned.1.call-start = ((), (), s32[]{:S(2)}) async-start(), calls=%async_computation.2 | async-start | bytes 262144 | tf_op jit(solution)/shard_map/psum | solution.py:72
  446.0 139.1 %all-gather.2.cloned.1.call-start = ((), (), s32[]{:S(2)}) async-start(), calls=%async_computation.3 | async-start | bytes 2162688 | tf_op jit(solution)/shard_map/all_gather | solution.py:76
  526.9 64.4 %copy-start.4 = (s32[1024]{0:T(1024)S(1)}, s32[1024]{0:T(1024)}, u32[]{:S(2)}) copy-start(s32[1024]{0:T(1024)} %param.13) | copy-start | bytes 12292
Sparse Core Ops, SparseCore 0:
  15.4 270.7 all-reduce.4
  374.8 67.3 all-reduce.6
  446.2 76.4 all-reduce.8
  526.0 59.1 all-gather.1
where the time goes:
time: 676 us
  waiting for transfers between devices  472 us (70%)
  blocking collectives  159 us (24%)
  matrix products  18 us (3%)
  between operations  16.2 us (2%)
  other arithmetic  7.64 us (1%)
    psum x1, waiting for transfers between devices, on_device(): summed = lax.psum(partial_sum, ('neur', 'tm'))  269 us
    psum x1, waiting for transfers between devices, on_device(): final_state = mixed_state + lax.psum(mlp_part, 'tm')  76.6 us
    psum x1, blocking collectives, on_device(): lax.psum((jnp.sum(gained), jnp.sum(heldout * counts)), ('neur', 'tm'))  74.4 us
    psum x1, waiting for transfers between devices, on_device(): mixed_state = stream + lax.psum(attn_part, 'tm')  67.4 us
    all_gather x1, waiting for transfers between devices, on_device(): lax.all_gather(latents, 'neur', axis=0, tiled=True)  58.2 us
    all_gather x1, blocking collectives, on_device(): lax.all_gather(keys_local, 'neur', axis=0, tiled=True)  42.8 us
    all_gather x1, blocking collectives, on_device(): lax.all_gather(values_local, 'neur', axis=0, tiled=True)  42.1 us
  transfers between devices with their start and end apart: 4, of which 4 were waited for; matrix products, arithmetic and copies ran while one was open for 1% of the time, Pallas kernels for 0%

commit v1 on v0

--- a/solution.py
+++ b/solution.py
@@ -31,7 +31,7 @@
     heldout = (1 - held_in).astype(jnp.float32)
     counts = jnp.sum(spikes, 0).astype(jnp.float32)
     partial_sum = jnp.dot(masked, readin_weight, preferred_element_type=jnp.float32)
-    summed = lax.psum(partial_sum, ("neur", "tm"))
+    summed = lax.psum(lax.psum(partial_sum, "neur"), "tm")
     stream = lax.dynamic_slice_in_dim(summed, lax.axis_index("neur") * rows_here, rows_here, 0)
     model_dim = stream.shape[1]
     head_cols = qkv_weight.shape[2]

time: 676 us -> 899 us (1.33)
  waiting for transfers between devices: 472 us -> 694 us
    psum x1 -> x2, waiting for transfers between devices: 269 us -> 491 us  [on_device(): summed = lax.psum(lax.psum(partial_sum, 'neur'), 'tm')]
  transfers between devices with their start and end apart: 4 -> 5, of which waited for: 4 -> 5; matrix products, arithmetic and copies ran while one was open for 1% -> 0% of each run, Pallas kernels for 0% -> 0%
where the time goes in v1:
time: 899 us
  waiting for transfers between devices  694 us (77%)
  blocking collectives  160 us (18%)
  matrix products  17.9 us (2%)
  between operations  16.2 us (2%)
    psum x2, waiting for transfers between devices, on_device(): summed = lax.psum(lax.psum(partial_sum, 'neur'), 'tm')  491 us
    psum x1, waiting for transfers between devices, on_device(): final_state = mixed_state + lax.psum(mlp_part, 'tm')  76.6 us
    psum x1, blocking collectives, on_device(): lax.psum((jnp.sum(gained), jnp.sum(heldout * counts)), ('neur', 'tm'))  74.3 us
    psum x1, waiting for transfers between devices, on_device(): mixed_state = stream + lax.psum(attn_part, 'tm')  68.4 us
    all_gather x1, waiting for transfers between devices, on_device(): lax.all_gather(latents, 'neur', axis=0, tiled=True)  57.9 us
    all_gather x1, blocking collectives, on_device(): lax.all_gather(keys_local, 'neur', axis=0, tiled=True)  45.7 us
    all_gather x1, blocking collectives, on_device(): lax.all_gather(values_local, 'neur', axis=0, tiled=True)  39.9 us
  transfers between devices with their start and end apart: 5, of which 5 were waited for; matrix products, arithmetic and copies ran while one was open for 0% of the time, Pallas kernels for 0%

profile of v1, /device:TPU:1, one launch (start us, length us, event | category | flops | bytes accessed | tf_op | source)
XLA Modules:
  0.0 898.8 jit_solution(16339645389753368060)
XLA Ops:
  7.2 0.0 copy-start
  7.2 0.0 all-reduce.6.cloned.1.call-start
  7.2 1.5 copy-done
  8.8 6.4 fusion
  15.2 0.0 copy-start.2
  15.2 0.0 all-reduce.6.cloned.1.call-update
  15.2 0.0 copy-start.1
  15.2 0.0 all-reduce.8.cloned.1.call-start
  15.3 302.8 %all-reduce.6.cloned.1.call-done = f32[1024,1024]{1,0:T(8,128)} async-done(((f32[1024,1024]{1,0:T(8,128)}), f32[1024,1024]{1,0:T(8,128)}) %all-reduce.6.cloned.1.call-update) | async-done | bytes 4194320 | tf_op jit(solution)/shard_map/psum | solution.py:34
  318.1 0.0 copy-start.5
  318.1 0.0 all-reduce.8.cloned.1.call-update
  318.1 0.0 copy-start.3
  318.1 0.0 all-reduce.10.cloned.1.call-start
  318.2 1.4 copy.15
  319.6 188.2 %all-reduce.8.cloned.1.call-done = f32[1024,1024]{1,0:T(8,128)} async-done(((f32[1024,1024]{1,0:T(8,128)}), f32[1024,1024]{1,0:T(8,128)}) %all-reduce.8.cloned.1.call-update) | async-done | bytes 4194320 | tf_op jit(solution)/shard_map/psum | solution.py:34
  507.8 1.0 multiply_reduce_fusion.2
  508.8 0.0 copy-done.2
  508.8 1.2 convolution_convert_fusion
  510.1 45.7 %all_gather.10 = bf16[1024,128]{1,0:T(8,128)(2,1)S(1)} all-gather(bf16[32,128]{1,0:T(8,128)(2,1)S(1)} %get-tuple-element.11), channel_id=1, replica_groups=mesh['neur'=32,'tm'=8] {'neur'}, dimensions={0}, use_global_device_ids=true | all-gather | bytes 270336 | tf_op jit(solution)/shard_map/all_gather | solution.py:47
  555.7 0.3 fusion.38
  556.0 39.9 %all_gather.9 = bf16[1024,128]{1,0:T(8,128)(2,1)S(1)} all-gather(bf16[32,128]{1,0:T(8,128)(2,1)S(1)} %get-tuple-element.12), channel_id=1, replica_groups=mesh['neur'=32,'tm'=8] {'neur'}, dimensions={0}, use_global_device_ids=true | all-gather | bytes 270336 | tf_op jit(solution)/shard_map/all_gather | solution.py:50
  595.9 0.0 copy-done.1
  595.9 0.0 copy-start.6
  595.9 0.9 fusion.6
  596.9 0.0 all-reduce.10.cloned.1.call-update
  596.9 0.0 all-reduce.12.cloned.1.call-start
  597.0 68.4 %all-reduce.10.cloned.1.call-done = f32[32,1024]{1,0:T(8,128)} async-done(((f32[32,1024]{1,0:T(8,128)}), f32[32,1024]{1,0:T(8,128)}) %all-reduce.10.cloned.1.call-update) | async-done | bytes 131088 | tf_op jit(solution)/shard_map/psum | solution.py:66
  665.4 1.1 multiply_reduce_fusion.1
  666.5 0.0 copy-done.5
  666.5 2.8 fusion.16
  669.3 0.0 all-reduce.12.cloned.1.call-update
  669.3 0.0 all-gather.2.cloned.1.call-start
  669.4 76.6 %all-reduce.12.cloned.1.call-done = f32[32,1024]{1,0:T(8,128)} async-done(((f32[32,1024]{1,0:T(8,128)}), f32[32,1024]{1,0:T(8,128)}) %all-reduce.12.cloned.1.call-update) | async-done | bytes 131088 | tf_op jit(solution)/shard_map/psum | solution.py:72
  745.9 1.0 multiply_reduce_fusion
  747.0 0.0 copy-done.3
  747.0 0.7 multiply_convert_fusion.2
  747.7 0.0 all-gather.2.cloned.1.call-update
  747.7 2.5 reduce_sum.77
  750.2 0.0 copy-start.4
  750.2 57.9 %all-gather.2.cloned.1.call-done = bf16[1024,1024]{1,0:T(8,128)(2,1)} async-done(((bf16[32,1024]{1,0:T(8,128)(2,1)}), bf16[1024,1024]{1,0:T(8,128)(2,1)}) %all-gather.2.cloned.1.call-update) | async-done | bytes 2097168 | tf_op jit(solution)/shard_map/all_gather | solution.py:76
  808.1 0.0 copy-done.6
  808.1 6.2 subtract_reduce_fusion
  814.3 0.0 copy-done.4
  814.3 1.3 multiply_reduce_fusion.3
  815.6 74.3 %all-reduce = (f32[]{:T(128)}, f32[]{:T(128)}) all-reduce(f32[]{:T(128)} %get-tuple-element.4, f32[]{:T(128)} %get-tuple-element.3), channel_id=1, replica_groups=mesh['neur'=32,'tm'=8] {'neur','tm'}, use_global_device_ids=true, to_apply=%region_11.0 | all-reduce | flops 2 | bytes 16 | tf_op jit(solution)/shard_map/psum | solution.py:88
  (4 shorter events, 0.0 us)
Async XLA Ops:
  7.2 1.6 copy-start
  7.2 310.9 %all-reduce.6.cloned.1.call-start = ((), (), s32[]{:S(2)}) async-start(), calls=%async_computation | async-start | bytes 8388608 | tf_op jit(solution)/shard_map/psum | solution.py:34
  15.2 493.6 %copy-start.2 = (f32[1024]{0:T(1024)S(1)}, f32[1024]{0:T(1024)}, u32[]{:S(2)}) copy-start(f32[1024]{0:T(1024)} %param.19) | copy-start | bytes 12292
  15.2 580.7 %copy-start.1 = (bf16[128,1024]{1,0:T(8,128)(2,1)S(1)}, bf16[128,1024]{1,0:T(8,128)(2,1)}, u32[]{:S(2)}) copy-start(bf16[128,1024]{1,0:T(8,128)(2,1)} %param.16) | copy-start | bytes 786436
  15.2 492.5 %all-reduce.8.cloned.1.call-start = ((), (), s32[]{:S(2)}) async-start(), calls=%async_computation.1 | async-start | bytes 8388608 | tf_op jit(solution)/shard_map/psum | solution.py:34
  318.1 348.4 %copy-start.5 = (f32[1024]{0:T(1024)S(1)}, f32[1024]{0:T(1024)}, u32[]{:S(2)}) copy-start(f32[1024]{0:T(1024)} %param.20) | copy-start | bytes 12292
  318.1 428.9 %copy-start.3 = (f32[1024]{0:T(1024)S(1)}, f32[1024]{0:T(1024)}, u32[]{:S(2)}) copy-start(f32[1024]{0:T(1024)} %param.21) | copy-start | bytes 12292
  318.1 347.3 %all-reduce.10.cloned.1.call-start = ((), (), s32[]{:S(2)}) async-start(), calls=%async_computation.2 | async-start | bytes 262144 | tf_op jit(solution)/shard_map/psum | solution.py:66
  595.9 212.1 %copy-start.6 = (f32[1024]{0:T(1024)S(1)}, f32[1024]{0:T(1024)}, u32[]{:S(2)}) copy-start(f32[1024]{0:T(1024)} %param.23) | copy-start | bytes 12292
  596.9 149.0 %all-reduce.12.cloned.1.call-start = ((), (), s32[]{:S(2)}) async-start(), calls=%async_computation.3 | async-start | bytes 262144 | tf_op jit(solution)/shard_map/psum | solution.py:72
  669.3 138.8 %all-gather.2.cloned.1.call-start = ((), (), s32[]{:S(2)}) async-start(), calls=%async_computation.4 | async-start | bytes 2162688 | tf_op jit(solution)/shard_map/all_gather | solution.py:76
  750.2 64.1 %copy-start.4 = (s32[1024]{0:T(1024)S(1)}, s32[1024]{0:T(1024)}, u32[]{:S(2)}) copy-start(s32[1024]{0:T(1024)} %param.13) | copy-start | bytes 12292
Sparse Core Ops, SparseCore 0:
  15.4 302.6 all-reduce.5
  320.7 186.9 all-reduce.7
  597.0 68.2 all-reduce.9
  669.4 76.4 all-reduce.11
  748.9 59.1 all-gather.1
